TPU v7x, 256 devices: a whole 4x4x8 slice. The times are simulated.
256 devices in a mesh: users: 64 (over z, y, core), items: 4 (over x).
Axes of the slice: x: 4, y: 4, z: 8, core: 2. Of those that a mesh axis runs over, the one named last changes fastest.
Arguments:
- user_factor: bfloat16 [131072, 256], P('users'), may hold values from -2.390625 to 2.390625
- hot_factor: bfloat16 [512, 256], replicated, may hold values from -2.390625 to 2.390625
- cold_factor: bfloat16 [65536, 256], P(('users', 'items')), may hold values from -2.390625 to 2.390625
- hour_factor: bfloat16 [168, 256], replicated, may hold values from -2.390625 to 2.390625
- block_user: int32 [256, 512], P(('users', 'items')), may hold values from 0 to 2047
- block_slot: int32 [256, 512], P(('users', 'items')), may hold values from 0 to 159
- block_hour: int32 [256, 512], P(('users', 'items')), may hold values from 0 to 20
- block_count: int32 [256], P(('users', 'items')), may hold values from 128 to 512, as said below
- need_rows: int32 [256, 64, 2], P(('users', 'items')), may hold values from 0 to 15
- observed: bfloat16 [256, 512, 128], P(('users', 'items')), may hold values from 0 to 1, as said below
Outputs:
- user_grad: float32 [131072, 256], P(('users', 'items'))
- cold_grad: float32 [65536, 256], P(('users', 'items'))
- hot_grad: float32 [512, 256], P(('users', 'items'))
- hour_grad: float32 [168, 256], replicated
Inputs may be any that keep to these rules, and one draw needn't show every extreme that they name: `block_count`: some device has all 512 slots live. `observed`: every entry is 0 or 1.
All inputs are finite; a program needn't handle non-finite values.
Results may differ from a plain program's by a relative error of at most 0.0029.
Values may be sent and summed in bfloat16 or wider, within the bound.
A program may use at most 128 MiB of HBM per device.

v0:
```python
import jax
import jax.numpy as jnp
from jax import lax
from jax.sharding import PartitionSpec as P

IB = 16
HB = 8


def body(
    user_factor,
    hot_factor,
    cold_factor,
    hour_factor,
    block_user,
    block_slot,
    block_hour,
    block_count,
    need_rows,
    observed,
):
    rank_size = user_factor.shape[1]
    hour_count = hour_factor.shape[0]
    hour_blocks = hour_count // HB
    hot_rows = hot_factor.shape[0]
    shard_len = cold_factor.shape[0]
    peer_count = lax.axis_size("users")
    requests = need_rows[0]
    offsets = jnp.arange(IB, dtype=jnp.int32)
    gathered = lax.all_gather(cold_factor, "users", axis=0, tiled=True)
    wanted_rows = (
        jnp.arange(peer_count, dtype=jnp.int32)[:, None, None] * shard_len
        + requests[:, :, None] * IB
        + offsets
    ).reshape(-1)
    fetched = gathered[wanted_rows]
    item_table = jnp.concatenate([hot_factor, fetched], axis=0)
    hour_table = hour_factor.reshape(hour_blocks, HB * rank_size)
    block_total = block_user.shape[1]
    group_len = min(block_total, 512)
    groups = block_total // group_len
    live_count = block_count[0]
    data = (
        block_user[0].reshape(groups, group_len),
        block_slot[0].reshape(groups, group_len),
        block_hour[0].reshape(groups, group_len),
        jnp.arange(block_total, dtype=jnp.int32).reshape(groups, group_len),
        observed[0].reshape(groups, group_len, IB, HB),
    )
    block_ids = jnp.arange(hour_blocks, dtype=jnp.int32)

    def one_group(carry, group_data):
        grad_user, grad_item, grad_hour = carry
        users_idx, slots_idx, hours_idx, position, obs = group_data
        user_rows = user_factor[users_idx]
        item_idx = slots_idx[:, None] * IB + offsets
        item_rows = item_table[item_idx]
        hour_onehot = (hours_idx[:, None] == block_ids).astype(jnp.bfloat16)
        hour_rows = jnp.dot(hour_onehot, hour_table, preferred_element_type=jnp.float32)
        hour_rows = hour_rows.astype(jnp.bfloat16).reshape(group_len, HB, rank_size)
        user_item = (
            user_rows.astype(jnp.float32)[:, None, :] * item_rows.astype(jnp.float32)
        ).astype(jnp.bfloat16)
        model = jnp.einsum("gar,gbr->gab", user_item, hour_rows, preferred_element_type=jnp.float32)
        live_mask = position < live_count
        residual = jnp.where(
            live_mask[:, None, None], jax.nn.sigmoid(model) - obs.astype(jnp.float32), 0.0
        )
        residual = residual.astype(jnp.bfloat16)
        weighted = jnp.einsum(
            "gab,gbr->gar", residual, hour_rows, preferred_element_type=jnp.float32
        )
        item_terms = weighted * user_rows.astype(jnp.float32)[:, None, :]
        user_terms = jnp.sum(weighted * item_rows.astype(jnp.float32), axis=1)
        hour_terms = jnp.einsum(
            "gab,gar->gbr", residual, user_item, preferred_element_type=jnp.float32
        )
        grad_user = grad_user.at[users_idx].add(user_terms)
        grad_item = grad_item.at[item_idx.reshape(-1)].add(item_terms.reshape(-1, rank_size))
        grad_hour = grad_hour.at[hours_idx].add(hour_terms.reshape(group_len, HB * rank_size))
        return ((grad_user, grad_item, grad_hour), None)

    start = (
        jnp.zeros((user_factor.shape[0], rank_size), jnp.float32),
        jnp.zeros((item_table.shape[0], rank_size), jnp.float32),
        jnp.zeros((hour_blocks, HB * rank_size), jnp.float32),
    )
    (grad_user, grad_item, grad_hour), _ = lax.scan(one_group, start, data)
    cold_part = grad_item[hot_rows:]
    dense_terms = (
        jnp.zeros((peer_count * shard_len, rank_size), jnp.float32).at[wanted_rows].add(cold_part)
    )
    cold_grad = lax.psum_scatter(dense_terms, "users", scatter_dimension=0, tiled=True)
    hot_grad = lax.psum_scatter(
        grad_item[:hot_rows], ("users", "items"), scatter_dimension=0, tiled=True
    )
    user_grad = lax.psum_scatter(grad_user, "items", scatter_dimension=0, tiled=True)
    hour_grad = lax.psum(grad_hour, ("users", "items")).reshape(hour_count, rank_size)
    return (user_grad, cold_grad, hot_grad, hour_grad)


def solution(mesh):
    in_specs = (
        P("users", None),
        P(),
        P(("users", "items"), None),
        P(),
        P(("users", "items"), None),
        P(("users", "items"), None),
        P(("users", "items"), None),
        P(("users", "items")),
        P(("users", "items"), None, None),
        P(("users", "items"), None, None),
    )
    out_specs = (
        P(("users", "items"), None),
        P(("users", "items"), None),
        P(("users", "items"), None),
        P(),
    )
    return jax.shard_map(body, mesh=mesh, in_specs=in_specs, out_specs=out_specs, check_vma=False)
```

profile of v0, /device:TPU:6, one launch (start us, length us, event | category | flops | bytes accessed | tf_op | source)
XLA Modules:
  0.0 702.9 jit_solution(4450357891006991247)
XLA Ops:
  7.2 0.0 copy-start
  7.2 0.0 copy-start.6
  7.2 0.0 all-gather.2.cloned.1.call-start
  7.2 0.7 all-gather.2.cloned.1.call-update
  7.9 0.0 all-reduce.4.cloned.1.call-start
  8.6 0.7 bitcast_add_fusion
  9.3 0.1 copy.18
  9.4 0.1 iota_add_fusion.1
  9.5 0.1 add.165
  9.7 1.0 reshape.237
  10.7 1.0 copy.19
  11.7 0.7 compare_select_fusion.4
  12.4 0.0 copy-done
  12.4 2.0 gather_fusion
  14.3 0.0 copy-start.5
  14.4 0.0 copy-done.6
  14.4 0.1 iota_add_fusion
  14.6 0.1 add.175
  14.7 0.1 compare_select_fusion
  14.8 0.1 reshape.261
  15.0 2.0 copy.20
  17.0 0.0 copy-done.5
  17.0 0.8 convolution_convert_fusion
  17.8 2.1 copy.21
  19.9 0.0 copy-start.4
  19.9 76.8 %all-gather.2.cloned.1.call-done = bf16[16384,256]{1,0:T(8,128)(2,1)} async-done(((bf16[256,256]{1,0:T(8,128)(2,1)}), bf16[16384,256]{1,0:T(8,128)(2,1)}) %all-gather.2.cloned.1.call-update) | async-done | bytes 8388624 | tf_op jit(solution)/shard_map/all_gather | solution.py:30
  96.7 11.1 %gather_fusion.1 = bf16[2048,256]{1,0:T(8,128)(2,1)S(1)} fusion(bf16[16384,256]{1,0:T(8,128)(2,1)} %all-gather.2.cloned.1.call-done, s32[2048]{0:T(1024)S(1)} %broadcast_clamp_fusion.1), kind=kCustom, calls=%fused_computation.1 | custom fusion | bytes 2105344 | tf_op jit(solution)/shard_map/gather | solution.py:36
  107.8 0.0 copy-done.4
  107.8 0.1 pad_maximum_fusion
  107.9 32.9 %gather_fusion.2 = bf16[8192,256]{1,0:T(8,128)(2,1)} fusion(bf16[2560,256]{1,0:T(8,128)(2,1)S(1)} %pad_maximum_fusion, s32[8192]{0:T(1024)S(1)} %broadcast_clamp_fusion), kind=kCustom, calls=%fused_computation.2 | custom fusion | bytes 8421376 | tf_op jit(solution)/shard_map/while/body/eval_jaxpr/gather | solution.py:57
  140.8 0.0 copy-start.2
  140.8 5.0 select_convert_fusion
  145.9 0.0 copy-done.2
  145.9 0.0 copy-start.3
  145.9 1.0 fusion.4
  146.8 0.6 copy-done.3
  147.5 5.1 broadcast_multiply_fusion
  152.6 3.9 copy.22
  156.5 8.7 %scatter_custom_fusion.3 = f32[21,2048]{1,0:T(8,128)S(1)} fusion(s32[512]{0:T(512)S(1)} %bitcast.48, f32[512,2048]{1,0:T(8,128)} %bitcast.39, f32[]{:T(128)} %constant.13.clone.1), kind=kCustom, calls=%fused_computation.30 | custom fusion | flops 1048576 | bytes 172544 | tf_op jit(solution)/shard_map/while/body/eval_jaxpr/scatter-add | solution.py:80
  165.2 0.7 reshape.241
  165.9 46.2 %scatter_custom_fusion.1 = f32[2560,256]{1,0:T(8,128)} fusion(s32[8192]{0:T(1024)S(1)} %bitcast.40, f32[8192,256]{1,0:T(8,128)} %bitcast.35, f32[]{:T(128)} %constant.13.clone.1), kind=kCustom, calls=%fused_computation.20 | custom fusion | flops 2097152 | bytes 2621952 | tf_op jit(solution)/shard_map/while/body/eval_jaxpr/scatter-add | solution.py:79
  212.1 1.9 slice.15
  214.0 0.0 all-reduce.4.cloned.1.call-update
  214.0 0.0 reduce-scatter.3.cloned.1.call-start
  214.1 4.9 scatter_custom_fusion
  219.0 0.0 reduce-scatter.3.cloned.1.call-update
  219.0 0.0 reduce-scatter.5.cloned.1.call-start
  219.1 18.9 %scatter_custom_fusion.2 = f32[16384,256]{1,0:T(8,128)} fusion(s32[2048]{0:T(1024)S(1)} %bitcast.42, f32[]{:T(128)} %constant.13.clone.1, f32[2560,256]{1,0:T(8,128)} %scatter_custom_fusion.1), kind=kCustom, calls=%fused_computation.11 | custom fusion | flops 524288 | bytes 18874880 | tf_op jit(solution)/shard_map/scatter-add | solution.py:91
  237.9 0.0 reduce-scatter.5.cloned.1.call-update
  238.0 0.0 copy-start.1
  238.0 229.4 %all-reduce.4.cloned.1.call-done = (f32[512,256]{1,0:T(8,128)}, f32[168,256]{1,0:T(8,128)}) async-done(((f32[512,256]{1,0:T(8,128)}, f32[168,256]{1,0:T(8,128)}), (f32[512,256]{1,0:T(8,128)}, f32[168,256]{1,0:T(8,128)})) %all-reduce.4.cloned.1.call-update) | async-done | bytes 696336
  467.4 1.3 constant_dynamic-slice_fusion
  468.6 29.8 %reduce-scatter.3.cloned.1.call-done = f32[512,256]{1,0:T(8,128)} async-done(((f32[2048,256]{1,0:T(8,128)}), f32[512,256]{1,0:T(8,128)}) %reduce-scatter.3.cloned.1.call-update) | async-done | bytes 524304 | tf_op jit(solution)/shard_map/reduce_scatter | solution.py:97
  498.4 196.4 %reduce-scatter.5.cloned.1.call-done = f32[256,256]{1,0:T(8,128)} async-done(((f32[16384,256]{1,0:T(8,128)}), f32[256,256]{1,0:T(8,128)}) %reduce-scatter.5.cloned.1.call-update) | async-done | bytes 262160 | tf_op jit(solution)/shard_map/reduce_scatter | solution.py:93
  694.8 1.6 copy.26
  696.4 0.0 copy-done.1
  (11 shorter events, 0.1 us)
Async XLA Ops:
  7.2 5.2 copy-start
  7.2 7.2 %copy-start.6 = (s32[1,512]{1,0:T(1,128)S(1)}, s32[1,512]{1,0:T(1,128)}, u32[]{:S(2)}) copy-start(s32[1,512]{1,0:T(1,128)} %param.15) | copy-start | bytes 6148
  7.2 89.5 %all-gather.2.cloned.1.call-start = ((), (), s32[]{:S(2)}) async-start(), calls=%async_computation.2 | async-start | bytes 8519680 | tf_op jit(solution)/shard_map/all_gather | solution.py:30
  7.9 459.4 %all-reduce.4.cloned.1.call-start = ((), (), s32[]{:S(2)}) async-start(), calls=%async_computation.5 | async-start | bytes 1392640
  14.3 2.7 copy-start.5
  19.9 87.9 %copy-start.4 = (bf16[512,256]{1,0:T(8,128)(2,1)S(1)}, bf16[512,256]{1,0:T(8,128)(2,1)}, u32[]{:S(2)}) copy-start(bf16[512,256]{1,0:T(8,128)(2,1)} %param.11) | copy-start | bytes 786436
  140.8 5.0 copy-start.2
  145.9 1.6 copy-start.3
  214.0 284.4 %reduce-scatter.3.cloned.1.call-start = ((), (), s32[]{:S(2)}) async-start(), calls=%async_computation.3 | async-start | bytes 2621440 | tf_op jit(solution)/shard_map/reduce_scatter | solution.py:97
  219.0 475.8 %reduce-scatter.5.cloned.1.call-start = ((), (), s32[]{:S(2)}) async-start(), calls=%async_computation.4 | async-start | bytes 17039360 | tf_op jit(solution)/shard_map/reduce_scatter | solution.py:93
  238.0 458.4 %copy-start.1 = (bf16[2048,256]{1,0:T(8,128)(2,1)S(1)}, bf16[2048,256]{1,0:T(8,128)(2,1)}, u32[]{:S(2)}) copy-start(bf16[2048,256]{1,0:T(8,128)(2,1)} %param.10) | copy-start | bytes 3145732
Sparse Core Ops, SparseCore 0:
  10.8 85.8 all-gather.1
  214.2 253.1 all-reduce.3
  470.5 27.8 reduce-scatter.2
  503.3 191.4 reduce-scatter.4
where the time goes:
time: 703 us
  waiting for transfers between devices  533 us (76%)
  other arithmetic  80.7 us (11%)
  local copies, waits for them, and re-layouts  62.5 us (9%)
  between operations  14.7 us (2%)
  matrix products  11.9 us (2%)
    unnamed x5, waiting for transfers between devices  230 us
    reduce_scatter x1, waiting for transfers between devices, body(): lax.psum_scatter(dense_terms, 'users', scatter_dimension=0, tiled=True)  196 us
    all_gather x1, waiting for transfers between devices, body(): gathered = lax.all_gather(cold_factor, 'users', axis=0, tiled=True)  76.8 us
    scatter-add x1, other arithmetic, one_group(): grad_item.at[item_idx.reshape(-1)].add(item_terms.reshape(-1, rank_size))  46.2 us
    gather x1, local copies, waits for them, and re-layouts, one_group(): item_rows = item_table[item_idx]  32.9 us
    reduce_scatter x1, waiting for transfers between devices, body(): lax.psum_scatter(grad_user, 'items', scatter_dimension=0, tiled=True)  29.8 us
    scatter-add x1, other arithmetic, body(): jnp.zeros((peer_count * shard_len, rank_size), jnp.float32).at[wanted_rows]  18.9 us
  transfers between devices with their start and end apart: 4, of which 4 were waited for; matrix products, arithmetic and copies ran while one was open for 5% of the time, Pallas kernels for 0%

commit v1 on v0

--- a/solution.py
+++ b/solution.py
@@ -5,6 +5,11 @@
 
 IB = 16
 HB = 8
+
+
+def exchange_gather(value, mesh_axis, dim):
+    stack = jnp.stack([value] * lax.axis_size(mesh_axis))
+    return jnp.concatenate(lax.all_to_all(stack, mesh_axis, 0, 0), axis=dim)
 
 
 def body(
@@ -27,7 +32,7 @@
     peer_count = lax.axis_size("users")
     requests = need_rows[0]
     offsets = jnp.arange(IB, dtype=jnp.int32)
-    gathered = lax.all_gather(cold_factor, "users", axis=0, tiled=True)
+    gathered = exchange_gather(cold_factor, "users", 0)
     wanted_rows = (
         jnp.arange(peer_count, dtype=jnp.int32)[:, None, None] * shard_len
         + requests[:, :, None] * IB

time: 703 us -> 610 us (0.87)
  waiting for transfers between devices: 533 us -> 420 us
  starting transfers between devices: 0.16 us -> 12.9 us
    reduce_scatter x1, waiting for transfers between devices: 196 us -> 0.01 us  [body(): lax.psum_scatter(dense_terms, 'users', scatter_dimension=0, tiled=True)]
    all_to_all x0 -> x1, waiting for transfers between devices: none -> 177 us  [exchange_gather(): return jnp.concatenate(lax.all_to_all(stack, mesh_axis, 0, 0), axis=dim)]
    all_gather x1 -> x0, waiting for transfers between devices: 76.8 us -> none  [body(): gathered = lax.all_gather(cold_factor, 'users', axis=0, tiled=True)]
    reduce_scatter x1, waiting for transfers between devices: 29.8 us -> 0.01 us  [body(): lax.psum_scatter(grad_user, 'items', scatter_dimension=0, tiled=True)]
    all_to_all x0 -> x1, starting transfers between devices: none -> 12.5 us  [exchange_gather(): return jnp.concatenate(lax.all_to_all(stack, mesh_axis, 0, 0), axis=dim)]
    unnamed x5 -> x4, waiting for transfers between devices: 230 us -> 242 us
  transfers between devices with their start and end apart: 4 -> 4, of which waited for: 4 -> 2; matrix products, arithmetic and copies ran while one was open for 5% -> 5% of each run, Pallas kernels for 0% -> 0%
where the time goes in v1:
time: 610 us
  waiting for transfers between devices  420 us (69%)
  other arithmetic  79 us (13%)
  local copies, waits for them, and re-layouts  67.8 us (11%)
  between operations  16.5 us (3%)
  matrix products  13.8 us (2%)
  starting transfers between devices  12.9 us (2%)
    unnamed x4, waiting for transfers between devices  242 us
    all_to_all x1, waiting for transfers between devices, exchange_gather(): return jnp.concatenate(lax.all_to_all(stack, mesh_axis, 0, 0), axis=dim)  177 us
    scatter-add x1, other arithmetic, one_group(): grad_item.at[item_idx.reshape(-1)].add(item_terms.reshape(-1, rank_size))  46.2 us
    gather x1, local copies, waits for them, and re-layouts, one_group(): item_rows = item_table[item_idx]  32.9 us
    scatter-add x1, other arithmetic, body(): jnp.zeros((peer_count * shard_len, rank_size), jnp.float32).at[wanted_rows]  18.9 us
    all_to_all x1, starting transfers between devices, exchange_gather(): return jnp.concatenate(lax.all_to_all(stack, mesh_axis, 0, 0), axis=dim)  12.5 us
  transfers between devices with their start and end apart: 4, of which 2 were waited for; matrix products, arithmetic and copies ran while one was open for 5% of the time, Pallas kernels for 0%

profile of v1, /device:TPU:6, one launch (start us, length us, event | category | flops | bytes accessed | tf_op | source)
XLA Modules:
  0.0 609.6 jit_solution(15623193032223122686)
XLA Ops:
  8.0 0.0 copy-start
  8.0 5.2 stack.2
  13.2 0.0 copy-start.10
  13.2 0.0 copy-start.8
  13.2 0.0 copy-start.9
  13.2 12.5 %all-to-all-start = ((bf16[64,256,256]{2,1,0:T(8,128)(2,1)}), bf16[64,256,256]{2,1,0:T(8,128)(2,1)}, u32[]{:S(2)}, u32[]{:S(2)}) async-start(bf16[64,256,256]{2,1,0:T(8,128)(2,1)} %stack.2), calls=%async_computation | async-start | bytes 16777216 | tf_op jit(solution)/shard_map/all_to_all | solution.py:12
  25.7 0.0 copy-start.6
  25.8 0.0 copy-start.7
  25.8 0.0 all-reduce.4.cloned.1.call-start
  25.8 0.0 copy-done.10
  25.9 0.1 copy.18
  26.0 0.1 iota_add_fusion.1
  26.1 0.1 add.165
  26.2 0.0 copy-done.8
  26.2 0.1 compare_select_fusion
  26.4 0.1 reshape.267
  26.5 0.0 copy-done.9
  26.6 0.0 copy-done
  26.6 2.0 gather_fusion
  28.6 0.0 copy-done.6
  28.6 0.1 reshape.243
  28.7 0.0 copy-done.7
  28.7 0.8 convolution_convert_fusion
  29.4 0.0 copy-start.5
  29.4 2.0 copy.21
  31.5 0.0 copy-done.5
  31.5 0.1 copy.19
  31.6 2.0 copy.20
  34.3 0.1 iota_add_fusion
  34.4 0.1 add.175
  34.7 177.3 %all-to-all-done = bf16[64,256,256]{2,1,0:T(8,128)(2,1)} async-done(((bf16[64,256,256]{2,1,0:T(8,128)(2,1)}), bf16[64,256,256]{2,1,0:T(8,128)(2,1)}, u32[]{:S(2)}, u32[]{:S(2)}) %all-to-all-start) | async-done | bytes 8388640 | tf_op jit(solution)/shard_map/all_to_all | solution.py:12
  211.9 0.0 copy-start.4
  211.9 11.1 %gather_fusion.1 = bf16[2048,256]{1,0:T(8,128)(2,1)S(1)} fusion(bf16[16384,256]{1,0:T(8,128)(2,1)} %bitcast.3, s32[2048]{0:T(1024)S(1)} %broadcast_clamp_fusion.1), kind=kCustom, calls=%fused_computation.1 | custom fusion | bytes 2105344 | tf_op jit(solution)/shard_map/gather | solution.py:41
  223.1 0.0 copy-done.4
  223.1 0.1 pad_maximum_fusion
  223.2 32.9 %gather_fusion.2 = bf16[8192,256]{1,0:T(8,128)(2,1)} fusion(bf16[2560,256]{1,0:T(8,128)(2,1)S(1)} %pad_maximum_fusion, s32[8192]{0:T(1024)S(1)} %broadcast_clamp_fusion), kind=kCustom, calls=%fused_computation.2 | custom fusion | bytes 8421376 | tf_op jit(solution)/shard_map/while/body/eval_jaxpr/gather | solution.py:62
  256.1 0.0 copy-start.2
  256.1 0.0 copy-start.3
  256.1 5.0 select_convert_fusion
  261.2 0.0 copy-done.2
  261.2 0.2 copy-done.3
  261.4 5.1 broadcast_multiply_fusion
  266.5 2.9 fusion.4
  269.4 46.2 %scatter_custom_fusion.1 = f32[2560,256]{1,0:T(8,128)} fusion(s32[8192]{0:T(1024)S(1)} %bitcast.41, f32[8192,256]{1,0:T(8,128)} %bitcast.36, f32[]{:T(128)} %constant.13.clone.1), kind=kCustom, calls=%fused_computation.20 | custom fusion | flops 2097152 | bytes 2621952 | tf_op jit(solution)/shard_map/while/body/eval_jaxpr/scatter-add | solution.py:84
  315.7 1.9 slice.15
  317.6 6.1 copy.22
  323.6 8.5 %scatter_custom_fusion.3 = f32[21,2048]{1,0:T(8,128)S(1)} fusion(s32[512]{0:T(512)S(1)} %bitcast.49, f32[512,2048]{1,0:T(8,128)} %bitcast.40, f32[]{:T(128)} %constant.13.clone.1), kind=kCustom, calls=%fused_computation.30 | custom fusion | flops 1048576 | bytes 172544 | tf_op jit(solution)/shard_map/while/body/eval_jaxpr/scatter-add | solution.py:85
  332.1 0.7 reshape.247
  332.8 0.0 all-reduce.4.cloned.1.call-update
  332.9 0.0 reduce-scatter.3.cloned.1.call-start
  332.9 4.7 scatter_custom_fusion
  337.6 0.0 reduce-scatter.3.cloned.1.call-update
  337.6 0.3 reduce-scatter.5.cloned.1.call-start
  337.9 18.9 %scatter_custom_fusion.2 = f32[16384,256]{1,0:T(8,128)} fusion(s32[2048]{0:T(1024)S(1)} %bitcast.43, f32[]{:T(128)} %constant.13.clone.1, f32[2560,256]{1,0:T(8,128)} %scatter_custom_fusion.1), kind=kCustom, calls=%fused_computation.11 | custom fusion | flops 524288 | bytes 18874880 | tf_op jit(solution)/shard_map/scatter-add | solution.py:96
  356.8 0.0 reduce-scatter.5.cloned.1.call-update
  356.9 0.0 copy-start.1
  356.9 242.4 %all-reduce.4.cloned.1.call-done = (f32[512,256]{1,0:T(8,128)}, f32[168,256]{1,0:T(8,128)}) async-done(((f32[512,256]{1,0:T(8,128)}, f32[168,256]{1,0:T(8,128)}), (f32[512,256]{1,0:T(8,128)}, f32[168,256]{1,0:T(8,128)})) %all-reduce.4.cloned.1.call-update) | async-done | bytes 696336
  599.3 1.3 constant_dynamic-slice_fusion
  600.6 0.0 reduce-scatter.3.cloned.1.call-done
  600.6 0.0 reduce-scatter.5.cloned.1.call-done
  600.6 1.6 copy.26
  602.2 0.0 copy-done.1
  (13 shorter events, 0.2 us)
Async XLA Ops:
  8.0 18.6 %copy-start = (bf16[2048,256]{1,0:T(8,128)(2,1)S(1)}, bf16[2048,256]{1,0:T(8,128)(2,1)}, u32[]{:S(2)}) copy-start(bf16[2048,256]{1,0:T(8,128)(2,1)} %param.10) | copy-start | bytes 3145732
  13.2 12.6 %copy-start.10 = (s32[1,64,2]{1,2,0:T(2,128)S(1)}, s32[1,64,2]{1,2,0:T(2,128)}, u32[]{:S(2)}) copy-start(s32[1,64,2]{1,2,0:T(2,128)} %param.18) | copy-start | bytes 1540
  13.2 13.0 %copy-start.8 = (s32[1,512]{1,0:T(1,128)S(1)}, s32[1,512]{1,0:T(1,128)}, u32[]{:S(2)}) copy-start(s32[1,512]{1,0:T(1,128)} %param.15) | copy-start | bytes 6148
  13.2 13.3 %copy-start.9 = (s32[1,512]{1,0:T(1,128)S(1)}, s32[1,512]{1,0:T(1,128)}, u32[]{:S(2)}) copy-start(s32[1,512]{1,0:T(1,128)} %param.14) | copy-start | bytes 6148
  13.2 198.7 %all-to-all-start = ((bf16[64,256,256]{2,1,0:T(8,128)(2,1)}), bf16[64,256,256]{2,1,0:T(8,128)(2,1)}, u32[]{:S(2)}, u32[]{:S(2)}) async-start(bf16[64,256,256]{2,1,0:T(8,128)(2,1)} %stack.2), calls=%async_computation | async-start | bytes 16777216 | tf_op jit(solution)/shard_map/all_to_all | solution.py:12
  25.7 2.8 copy-start.6
  25.8 2.9 copy-start.7
  25.8 573.6 %all-reduce.4.cloned.1.call-start = ((), (), s32[]{:S(2)}) async-start(), calls=%async_computation.5 | async-start | bytes 1392640
  29.4 2.0 copy-start.5
  211.9 11.2 %copy-start.4 = (bf16[512,256]{1,0:T(8,128)(2,1)S(1)}, bf16[512,256]{1,0:T(8,128)(2,1)}, u32[]{:S(2)}) copy-start(bf16[512,256]{1,0:T(8,128)(2,1)} %param.11) | copy-start | bytes 786436
  256.1 5.0 copy-start.2
  256.1 5.3 copy-start.3
  332.9 267.8 %reduce-scatter.3.cloned.1.call-start = ((), (), s32[]{:S(2)}) async-start(), calls=%async_computation.3 | async-start | bytes 2621440 | tf_op jit(solution)/shard_map/reduce_scatter | solution.py:102
  337.6 263.0 %reduce-scatter.5.cloned.1.call-start = ((), (), s32[]{:S(2)}) async-start(), calls=%async_computation.4 | async-start | bytes 17039360 | tf_op jit(solution)/shard_map/reduce_scatter | solution.py:98
  356.9 245.3 %copy-start.1 = (bf16[2048,256]{1,0:T(8,128)(2,1)S(1)}, bf16[2048,256]{1,0:T(8,128)(2,1)}, u32[]{:S(2)}) copy-start(bf16[2048,256]{1,0:T(8,128)(2,1)} %param.10) | copy-start | bytes 3145732
Sparse Core Ops, SparseCore 0:
  333.0 266.3 all-reduce.3
Sparse Core Ops, SparseCore 1:
  337.7 27.5 reduce-scatter.2
  370.2 191.6 reduce-scatter.4
